TPU v7x, 32 devices: a whole 2x2x4 slice. The times are simulated.
32 devices in a mesh: pair: 8 (over z, y), aux: 4 (over x, core).
Axes of the slice: x: 2, y: 2, z: 4, core: 2. Of those that a mesh axis runs over, the one named last changes fastest.
Arguments:
- amplitudes: float32 [896, 8, 896], P('aux', 'pair'), may hold values from -6 to 6
- fitting: float32 [4, 896, 896], P('aux', 'pair'), may hold values from -0.09375 to 0.09375
Outputs:
- ladder: float32 [896, 8, 896], P('aux', 'pair')
All inputs are finite; a program needn't handle non-finite values.
Results may differ from a plain program's by a relative error of at most 0.0001.
Values sent between devices are 32-bit elements; how exact they have to be, the bound alone decides.
A program may use at most 64 MiB of HBM per device.

v0:
```python
import jax
import jax.numpy as jnp
from jax import lax
from jax.sharding import PartitionSpec as P


def per_device(amplitudes, fitting):
    width = amplitudes.shape[2]
    pair_dev = amplitudes.shape[1]
    count_fit = fitting.shape[0]
    whole_fit = lax.all_gather(fitting, "pair", axis=1, tiled=True)
    whole_amp = lax.all_gather(amplitudes, "aux", axis=0, tiled=True)
    halves = jnp.einsum(
        "rpd,lbd->lrpb",
        whole_amp,
        whole_fit,
        precision=lax.Precision.HIGHEST,
        preferred_element_type=jnp.float32,
    )
    halves = halves.reshape(count_fit, width, pair_dev * width)
    result = lax.psum_scatter(
        jnp.einsum(
            "lac,lcx->ax",
            whole_fit,
            halves,
            precision=lax.Precision.HIGHEST,
            preferred_element_type=jnp.float32,
        ),
        "aux",
        scatter_dimension=0,
        tiled=True,
    )
    return result.reshape(result.shape[0], pair_dev, width)


def solution(mesh):
    in_specs = (P("aux", "pair", None), P("aux", "pair", None))
    out_specs = P("aux", "pair", None)
    return jax.shard_map(
        per_device, mesh=mesh, in_specs=in_specs, out_specs=out_specs, check_vma=False
    )
```

profile of v0, /device:TPU:0, one launch (start us, length us, event | category | flops | bytes accessed | tf_op | source)
XLA Modules:
  0.0 180.0 jit_solution(6608431639948401352)
XLA Ops:
  6.5 0.0 all-gather.5.cloned.1.call-start
  6.5 0.7 all-gather.5.cloned.1.call-update
  7.3 0.0 all-gather.3.cloned.1.call-start
  7.3 0.7 all-gather.3.cloned.1.call-update
  8.0 0.0 reduce-scatter.4.cloned.1.call-start
  8.1 32.5 %all-gather.5.cloned.1.call-done = f32[896,1,896]{2,1,0:T(1,128)} async-done(((f32[224,1,896]{2,1,0:T(1,128)}), f32[896,1,896]{2,1,0:T(1,128)}) %all-gather.5.cloned.1.call-update) | async-done | bytes 3211280 | tf_op jit(solution)/shard_map/all_gather | solution.py:12
  40.5 62.9 %all-gather.3.cloned.1.call-done = f32[1,896,896]{2,1,0:T(8,128)} async-done(((f32[1,112,896]{2,1,0:T(8,128)}), f32[1,896,896]{2,1,0:T(8,128)}) %all-gather.3.cloned.1.call-update) | async-done | bytes 3211280 | tf_op jit(solution)/shard_map/all_gather | solution.py:11
  103.4 0.0 copy-start
  103.4 14.9 %fusion = f32[896,896]{1,0:T(8,128)S(1)} fusion(f32[896,1,896]{2,1,0:T(1,128)} %all-gather.5.cloned.1.call-done, f32[1,896,896]{2,1,0:T(8,128)} %all-gather.3.cloned.1.call-done), kind=kOutput, calls=%fused_computation | convolution fusion | flops 8631877632 | bytes 9633792 | tf_op jit(solution)/shard_map/rpd,lbd->lrpb/dot_general | solution.py:13
  118.3 0.0 copy-done
  118.3 11.7 %fusion.7 = f32[896,896]{0,1:T(8,128)S(1)} fusion(f32[1,896,896]{2,1,0:T(8,128)S(1)} %copy-done, f32[896,896]{1,0:T(8,128)S(1)} %fusion), kind=kOutput, calls=%fused_computation.7 | convolution fusion | flops 8631877632 | bytes 9633792 | tf_op jit(solution)/shard_map/lac,lcx->ax/dot_general | solution.py:22
  129.9 3.0 %copy.5 = f32[896,896]{1,0:T(8,128)} copy(f32[896,896]{0,1:T(8,128)S(1)} %fusion.7) | data formatting | bytes 6422528
  133.0 0.0 reduce-scatter.4.cloned.1.call-update
  133.0 37.1 %reduce-scatter.4.cloned.1.call-done = f32[224,896]{1,0:T(8,128)} async-done(((f32[896,896]{1,0:T(8,128)}), f32[224,896]{1,0:T(8,128)}) %reduce-scatter.4.cloned.1.call-update) | async-done | bytes 802832
  170.1 1.4 copy.6
  171.5 1.9 %copy.4 = f32[224,1,896]{2,1,0:T(1,128)} copy(f32[224,1,896]{0,2,1:T(8,128)S(1)} %bitcast.23) | data formatting | bytes 1605632 | tf_op jit(solution)/shard_map/reshape | solution.py:33
Async XLA Ops:
  6.5 34.0 %all-gather.5.cloned.1.call-start = ((), (), s32[]{:S(2)}) async-start(), calls=%async_computation.2 | async-start | bytes 4014080 | tf_op jit(solution)/shard_map/all_gather | solution.py:12
  7.3 96.2 %all-gather.3.cloned.1.call-start = ((), (), s32[]{:S(2)}) async-start(), calls=%async_computation.1 | async-start | bytes 3612672 | tf_op jit(solution)/shard_map/all_gather | solution.py:11
  8.0 162.1 %reduce-scatter.4.cloned.1.call-start = ((), (), s32[]{:S(2)}) async-start(), calls=%async_computation.3 | async-start | bytes 4014080
  103.4 14.9 %copy-start = (f32[1,896,896]{2,1,0:T(8,128)S(1)}, f32[1,896,896]{2,1,0:T(8,128)}, u32[]{:S(2)}) copy-start(f32[1,896,896]{2,1,0:T(8,128)} %all-gather.3.cloned.1.call-done) | copy-start | bytes 9633796
Sparse Core Ops, SparseCore 0:
  8.9 31.5 all-gather.4
  42.7 60.6 all-gather.2
  133.1 36.9 reduce-scatter.3
where the time goes:
time: 180 us
  waiting for transfers between devices  134 us (74%)
  matrix products  26.5 us (15%)
  between operations  13.1 us (7%)
  local copies, waits for them, and re-layouts  6.39 us (4%)
    all_gather x1, waiting for transfers between devices, per_device(): whole_fit = lax.all_gather(fitting, 'pair', axis=1, tiled=True)  62.9 us
    unnamed x4, waiting for transfers between devices  38.5 us
    all_gather x1, waiting for transfers between devices, per_device(): whole_amp = lax.all_gather(amplitudes, 'aux', axis=0, tiled=True)  32.5 us
    dot_general x1, matrix products, per_device(): jnp.einsum('rpd,lbd->lrpb', whole_amp, whole_fit, precision=lax.Precision...  14.9 us
    dot_general x1, matrix products, per_device(): jnp.einsum('lac,lcx->ax', whole_fit, halves, precision=lax.Precision.HIGH...  11.7 us
    unnamed x4, local copies, waits for them, and re-layouts  4.45 us
  transfers between devices with their start and end apart: 3, of which 3 were waited for; matrix products, arithmetic and copies ran while one was open for 0% of the time, Pallas kernels for 0%

commit v1 on v0

v1 whole, which is shorter than its diff:
```python
import functools

import jax
import jax.numpy as jnp
from jax import lax
from jax.experimental import pallas as pl
from jax.experimental.pallas import tpu as pltpu
from jax.sharding import PartitionSpec as P

MESH = pl.DeviceIdType.MESH
F32, BF16 = jnp.float32, jnp.bfloat16
NT = (((1,), (1,)), ((), ()))


def ring_order(n):
    depth = 4 if n % 4 == 0 and n > 4 else 2
    width = n // depth
    if n % 2 or width < 2:
        return list(range(n))
    walk = []
    for z in range(depth):
        ys = range(1, width) if z % 2 == 0 else range(width - 1, 0, -1)
        walk += [z * width + y for y in ys]
    return walk + [z * width for z in range(depth - 1, -1, -1)]


def lookup(table, key):
    return sum(jnp.where(key == k, v, 0) for k, v in enumerate(table))


def split(v):
    high = v.astype(BF16).astype(F32)
    return high, v - high


def kernel(
    n, chips, parts, cut,
    t_in, b_in, out,
    t_all, b_all, t_high, t_low, b_high, b_low, g_all,
    mate_out, mate_in, sum_out, sum_in,
    local_sem, right_send, right_recv, left_send, left_recv,
    tx_send, tx_recv, tm_send, tm_recv, pm_send, pm_recv, px_send, px_recv,
):
    width = t_all.shape[1]
    rows_t, rows_b = t_in.shape[0], b_in.shape[0]
    piece = rows_t // parts
    reach = n // 2
    order = ring_order(n)
    where = [order.index(k) for k in range(n)]
    pair, aux = lax.axis_index("pair"), lax.axis_index("aux")
    chip, core = aux // 2, aux % 2
    mate = chip * 2 + (1 - core)
    spot = lookup(where, pair)

    def at(step):
        return lookup(order, lax.rem(spot + step + n, n))

    right, left = at(1), at(-1)

    def chip_at(step):
        return lax.rem(chip + step + chips, chips)

    barrier = pltpu.get_barrier_semaphore()
    greet = [(right, aux), (left, aux), (pair, mate)]
    greet += [(pair, chip_at(e) * 2 + core) for e in range(1, chips)]
    for who in greet:
        pl.semaphore_signal(barrier, inc=1, device_id=who, device_id_type=MESH)
    pl.semaphore_wait(barrier, len(greet))

    bounds = [(0, cut), (cut, rows_b - cut)]

    def b_rows(block, h):
        start, size = bounds[h]
        return pl.ds(pl.multiple_of(block * rows_b + start, 8), size)

    def t_rows(owner, s):
        return pl.ds(pl.multiple_of(owner * rows_t + s * piece, 8), piece)

    def hop(d, h, to_right):
        step = (1 - d) if to_right else (d - 1)
        block = at(step)
        rows = b_rows(block, h)
        start, size = bounds[h]
        src = b_in.at[pl.ds(start, size)] if d == 1 else b_all.at[rows]
        send, recv = (right_send, right_recv) if to_right else (left_send, left_recv)
        return pltpu.make_async_remote_copy(
            src_ref=src,
            dst_ref=b_all.at[rows],
            send_sem=send.at[d - 1, h],
            recv_sem=recv.at[d - 1, h],
            device_id=(right if to_right else left, aux),
            device_id_type=MESH,
        )

    def arrive(d, h, from_left):
        block = at(-d if from_left else d)
        rows = b_rows(block, h)
        send, recv = (right_send, right_recv) if from_left else (left_send, left_recv)
        pltpu.make_async_remote_copy(
            src_ref=b_all.at[rows],
            dst_ref=b_all.at[rows],
            send_sem=send.at[d - 1, h],
            recv_sem=recv.at[d - 1, h],
            device_id=(left if from_left else right, aux),
            device_id_type=MESH,
        ).wait_recv()

    def carried(d, h, to_right):
        return d < reach or (h == 0) == to_right

    def t_cross(e, s):
        return pltpu.make_async_remote_copy(
            src_ref=t_in.at[pl.ds(s * piece, piece)],
            dst_ref=t_all.at[t_rows(aux, s)],
            send_sem=tx_send.at[e - 1, s],
            recv_sem=tx_recv.at[e - 1, s],
            device_id=(pair, chip_at(e) * 2 + core),
            device_id_type=MESH,
        )

    def t_mate(e, s):
        rows = t_rows(chip_at(-e) * 2 + core, s)
        return pltpu.make_async_remote_copy(
            src_ref=t_in.at[pl.ds(s * piece, piece)] if e == 0 else t_all.at[rows],
            dst_ref=t_all.at[rows],
            send_sem=tm_send.at[e, s],
            recv_sem=tm_recv.at[e, s],
            device_id=(pair, mate),
            device_id_type=MESH,
        )

    def landed(ref, rows, send, recv):
        pltpu.make_async_remote_copy(
            src_ref=ref.at[rows], dst_ref=ref.at[rows], send_sem=send, recv_sem=recv,
            device_id=(pair, mate), device_id_type=MESH,
        ).wait_recv()

    started = []

    def go(copy):
        copy.start()
        started.append(copy)

    for h in range(2):
        for to_right in (True, False):
            if carried(1, h, to_right):
                go(hop(1, h, to_right))
    for s in range(parts):
        for e in range(1, chips):
            go(t_cross(e, s))
    for s in range(parts):
        go(t_mate(0, s))
    own_b = pltpu.make_async_copy(
        b_in, b_all.at[pl.ds(pl.multiple_of(pair * rows_b, 8), rows_b)], local_sem.at[0]
    )
    own_t = pltpu.make_async_copy(
        t_in, t_all.at[pl.ds(pl.multiple_of(aux * rows_t, 8), rows_t)], local_sem.at[1]
    )
    own_b.start()
    own_t.start()
    own_b.wait()
    own_t.wait()

    def relay(d):
        for h in range(2):
            for from_left in (True, False):
                if carried(d, h, from_left):
                    arrive(d, h, from_left)
                    if d < reach and carried(d + 1, h, from_left):
                        go(hop(d + 1, h, from_left))

    def t_relay(s):
        for e in range(1, chips):
            landed(
                t_all, t_rows(chip_at(-e) * 2 + core, s),
                tx_send.at[e - 1, s], tx_recv.at[e - 1, s],
            )
            go(t_mate(e, s))

    def first_product(block):
        rows = pl.ds(pl.multiple_of(block * rows_b, 8), rows_b)
        high, low = split(b_all[rows, :])
        if rows_b % 16 == 0:
            b_high[pl.ds(pl.multiple_of(block * rows_b, 16), rows_b), :] = high.astype(BF16)
            b_low[pl.ds(pl.multiple_of(block * rows_b, 16), rows_b), :] = low.astype(BF16)
        both = jnp.concatenate([high, low], axis=0).astype(BF16)
        main = jnp.dot(both, t_high[...], preferred_element_type=F32)
        rest = jnp.dot(high.astype(BF16), t_low[...], preferred_element_type=F32)
        g_all[rows, :] = main[:rows_b] + (main[rows_b:] + rest)

    early = max(1, reach - 2)
    for d in range(1, early + 1):
        relay(d)
        if d <= parts:
            t_relay(d - 1)
    for s in range(min(early, parts), parts):
        t_relay(s)
    for e in range(chips):
        for s in range(parts):
            landed(
                t_all, t_rows(chip_at(-e) * 2 + (1 - core), s),
                tm_send.at[e, s], tm_recv.at[e, s],
            )

    @pl.loop(0, width // 128)
    def _(i):
        rows = pl.ds(pl.multiple_of(i * 128, 128), 128)
        high, low = split(t_all[rows, :])
        t_high[rows, :] = high.astype(BF16)
        t_low[rows, :] = low.astype(BF16)

    @pl.loop(-(early - 1), early)
    def _(i):
        first_product(at(i))

    def both_sides(d):
        @pl.loop(0, 2)
        def _(i):
            first_product(at((2 * i - 1) * d))

    for d in range(early + 1, reach):
        relay(d)
        both_sides(d - 1)
    if reach > 1:
        both_sides(reach - 1)
    relay(reach)
    first_product(at(reach))

    if rows_b % 16:
        @pl.loop(0, width // 128)
        def _(i):
            rows = pl.ds(pl.multiple_of(i * 128, 128), 128)
            high, low = split(b_all[rows, :])
            b_high[rows, :] = high.astype(BF16)
            b_low[rows, :] = low.astype(BF16)

    def second_product(owner, s):
        high, low = split(g_all[t_rows(owner, s), :])
        both = jnp.concatenate([high, low], axis=0).astype(BF16)
        main = lax.dot_general(both, b_high[...], NT, preferred_element_type=F32)
        rest = lax.dot_general(high.astype(BF16), b_low[...], NT, preferred_element_type=F32)
        return main[:piece] + (main[piece:] + rest)

    def p_mate(e, s):
        return pltpu.make_async_remote_copy(
            src_ref=mate_out.at[e, s], dst_ref=mate_in.at[e, s],
            send_sem=pm_send.at[e, s], recv_sem=pm_recv.at[e, s],
            device_id=(pair, mate), device_id_type=MESH,
        )

    def p_cross(e, s):
        return pltpu.make_async_remote_copy(
            src_ref=sum_out.at[e - 1, s], dst_ref=sum_in.at[e - 1, s],
            send_sem=px_send.at[e - 1, s], recv_sem=px_recv.at[e - 1, s],
            device_id=(pair, chip_at(e) * 2 + core), device_id_type=MESH,
        )

    def chip_sum(e, s):
        mate_out[e, s] = second_product(chip_at(e) * 2 + (1 - core), s)
        p_mate(e, s).start()
        mine = second_product(chip_at(e) * 2 + core, s)
        p_mate(e, s).wait_recv()
        return mine + mate_in[e, s]

    @pl.loop(0, (chips - 1) * parts)
    def _(i):
        e, s = i // parts + 1, i % parts
        sum_out[e - 1, s] = chip_sum(e, s)
        p_cross(e, s).start()

    @pl.loop(0, parts)
    def _(s):
        out[pl.ds(pl.multiple_of(s * piece, 8), piece), :] = chip_sum(0, s)

    for s in range(parts):
        rows = pl.ds(s * piece, piece)
        for e in range(1, chips):
            p_cross(e, s).wait_recv()
            out[rows, :] += sum_in[e - 1, s]

    for copy in started:
        copy.wait_send()
    for e in range(chips):
        for s in range(parts):
            p_mate(e, s).wait_send()
            if e:
                p_cross(e, s).wait_send()


def per_device(n, n_aux, amplitudes, fitting):
    rows_t, pair_dev, width = amplitudes.shape
    count_fit, rows_b, _ = fitting.shape
    assert pair_dev == 1 and count_fit == 1
    chips = n_aux // 2
    parts = 2 if rows_t % 16 == 0 else 1
    piece = rows_t // parts
    cut = rows_b // 16 * 8
    reach = n // 2
    dma = pltpu.SemaphoreType.DMA
    whole_f32 = pltpu.VMEM((width, width), F32)
    whole_bf16 = pltpu.VMEM((width, width), BF16)
    blocks = lambda k: pltpu.VMEM((k, parts, piece, width), F32)
    result = pl.pallas_call(
        functools.partial(kernel, n, chips, parts, cut),
        out_shape=jax.ShapeDtypeStruct((rows_t, width), F32),
        in_specs=[pl.BlockSpec(memory_space=pl.ANY)] * 2,
        out_specs=pl.BlockSpec(memory_space=pltpu.VMEM),
        scratch_shapes=[
            whole_f32, whole_f32, whole_bf16, whole_bf16, whole_bf16, whole_bf16, whole_f32,
            blocks(chips), blocks(chips), blocks(chips - 1), blocks(chips - 1),
            dma((2,)),
            dma((reach, 2)), dma((reach, 2)), dma((reach, 2)), dma((reach, 2)),
            dma((chips - 1, parts)), dma((chips - 1, parts)),
            dma((chips, parts)), dma((chips, parts)),
            dma((chips, parts)), dma((chips, parts)),
            dma((chips - 1, parts)), dma((chips - 1, parts)),
        ],
        compiler_params=pltpu.CompilerParams(
            collective_id=0, has_side_effects=True, vmem_limit_bytes=60 << 20
        ),
    )(amplitudes.reshape(rows_t, width), fitting.reshape(rows_b, width))
    return result.reshape(rows_t, pair_dev, width)


def solution(mesh):
    spec = P("aux", "pair", None)
    return jax.shard_map(
        functools.partial(per_device, mesh.shape["pair"], mesh.shape["aux"]),
        mesh=mesh, in_specs=(spec, spec), out_specs=spec, check_vma=False,
    )
```

time: 180 us -> 66.8 us (0.37)
  waiting for transfers between devices: 134 us -> 0 us
  Pallas kernels: 0 us -> 61.7 us
  matrix products: 26.5 us -> 0 us
  between operations: 13.1 us -> 0.01 us
    all_gather x2 -> x0, waiting for transfers between devices: 95.4 us -> none  [the longest x1 62.9 us: per_device(): whole_fit = lax.all_gather(fitting, 'pair', axis=1, tiled=True)]
    pallas_call x0 -> x1, Pallas kernels: none -> 61.7 us  [per_device(): pl.pallas_call(functools.partial(kernel, n, chips, parts, cut), out_shape...]
    unnamed x4 -> x0, waiting for transfers between devices: 38.5 us -> none
    dot_general x2 -> x0, matrix products: 26.5 us -> none  [the longest x1 14.9 us: per_device(): jnp.einsum('rpd,lbd->lrpb', whole_amp, whole_fit, precision=lax.Precision...]
    unnamed x4 -> x1, local copies, waits for them, and re-layouts: 4.45 us -> 2.07 us
  transfers between devices with their start and end apart: 3 -> 0, of which waited for: 3 -> 0; matrix products, arithmetic and copies ran while one was open for 0% -> 0% of each run, Pallas kernels for 0% -> 0%
where the time goes in v1:
time: 66.8 us; the launch traced here: 66.6 us
  Pallas kernels  61.7 us (92%)
  local copies, waits for them, and re-layouts  4.92 us (7%)
    pallas_call x1, Pallas kernels, per_device(): pl.pallas_call(functools.partial(kernel, n, chips, parts, cut), out_shape...  61.7 us
    reshape x1, local copies, waits for them, and re-layouts, per_device(): return result.reshape(rows_t, pair_dev, width)  2.85 us
    unnamed x1, local copies, waits for them, and re-layouts  2.07 us

profile of v1, /device:TPU:0, one launch (start us, length us, event | category | flops | bytes accessed | tf_op | source)
XLA Modules:
  0.0 66.6 jit_solution(8173457854126383417)
XLA Ops:
  0.0 2.1 %copy.6 = f32[224,1,896]{2,0,1:T(8,128)} copy(f32[224,1,896]{2,1,0:T(1,128)} %param.2) | data formatting | bytes 1605632
  2.1 61.7 %shard_map.28 = f32[224,896]{1,0:T(8,128)} custom-call(f32[224,896]{1,0:T(8,128)} %bitcast.6, f32[112,896]{1,0:T(8,128)} %bitcast.7), custom_call_target="tpu_custom_call" | custom-call | tf_op jit(solution)/shard_map/pallas_call | solution.py:303
  63.8 2.8 %copy.3 = f32[224,1,896]{2,1,0:T(1,128)} copy(f32[224,1,896]{2,0,1:T(8,128)} %bitcast.5) | data formatting | bytes 1605632 | tf_op jit(solution)/shard_map/reshape | solution.py:322

commit v2 on v1

--- a/solution.py
+++ b/solution.py
@@ -8,6 +8,7 @@
 from jax.sharding import PartitionSpec as P
 
 MESH = pl.DeviceIdType.MESH
+CUTS, PARTS = 4, 4
 F32, BF16 = jnp.float32, jnp.bfloat16
 NT = (((1,), (1,)), ((), ()))
 
@@ -34,15 +35,17 @@
 
 
 def kernel(
-    n, chips, parts, cut,
+    n, chips, parts, cuts,
     t_in, b_in, out,
     t_all, b_all, t_high, t_low, b_high, b_low, g_all,
-    mate_out, mate_in, sum_out, sum_in,
+    mate_out, mate_in, sum_out, sum_in, kept,
     local_sem, right_send, right_recv, left_send, left_recv,
     tx_send, tx_recv, tm_send, tm_recv, pm_send, pm_recv, px_send, px_recv,
 ):
-    width = t_all.shape[1]
-    rows_t, rows_b = t_in.shape[0], b_in.shape[0]
+    rows_b, width = b_in.shape
+    lanes = t_in.shape[1]
+    tiles = width // lanes
+    rows_t = t_in.shape[0] // tiles
     piece = rows_t // parts
     reach = n // 2
     order = ring_order(n)
@@ -67,14 +70,22 @@
         pl.semaphore_signal(barrier, inc=1, device_id=who, device_id_type=MESH)
     pl.semaphore_wait(barrier, len(greet))
 
-    bounds = [(0, cut), (cut, rows_b - cut)]
+    edges = [rows_b // 8 * k // cuts * 8 for k in range(cuts)] + [rows_b]
+    bounds = [(a, b - a) for a, b in zip(edges, edges[1:])]
 
     def b_rows(block, h):
         start, size = bounds[h]
         return pl.ds(pl.multiple_of(block * rows_b + start, 8), size)
 
+    def g_rows(owner, s):
+        return pl.ds(pl.multiple_of(owner * rows_t + s * piece, 8), piece)
+
     def t_rows(owner, s):
-        return pl.ds(pl.multiple_of(owner * rows_t + s * piece, 8), piece)
+        start = (owner * rows_t + s * piece) * tiles
+        return pl.ds(pl.multiple_of(start, 8), piece * tiles)
+
+    def t_own(s):
+        return pl.ds(s * piece * tiles, piece * tiles)
 
     def hop(d, h, to_right):
         step = (1 - d) if to_right else (d - 1)
@@ -106,11 +117,11 @@
         ).wait_recv()
 
     def carried(d, h, to_right):
-        return d < reach or (h == 0) == to_right
+        return d < reach or (h < cuts // 2) == to_right
 
     def t_cross(e, s):
         return pltpu.make_async_remote_copy(
-            src_ref=t_in.at[pl.ds(s * piece, piece)],
+            src_ref=t_in.at[t_own(s)],
             dst_ref=t_all.at[t_rows(aux, s)],
             send_sem=tx_send.at[e - 1, s],
             recv_sem=tx_recv.at[e - 1, s],
@@ -121,7 +132,7 @@
     def t_mate(e, s):
         rows = t_rows(chip_at(-e) * 2 + core, s)
         return pltpu.make_async_remote_copy(
-            src_ref=t_in.at[pl.ds(s * piece, piece)] if e == 0 else t_all.at[rows],
+            src_ref=t_in.at[t_own(s)] if e == 0 else t_all.at[rows],
             dst_ref=t_all.at[rows],
             send_sem=tm_send.at[e, s],
             recv_sem=tm_recv.at[e, s],
@@ -141,7 +152,7 @@
         copy.start()
         started.append(copy)
 
-    for h in range(2):
+    for h in range(cuts):
         for to_right in (True, False):
             if carried(1, h, to_right):
                 go(hop(1, h, to_right))
@@ -154,7 +165,7 @@
         b_in, b_all.at[pl.ds(pl.multiple_of(pair * rows_b, 8), rows_b)], local_sem.at[0]
     )
     own_t = pltpu.make_async_copy(
-        t_in, t_all.at[pl.ds(pl.multiple_of(aux * rows_t, 8), rows_t)], local_sem.at[1]
+        t_in, t_all.at[pl.ds(pl.multiple_of(aux * rows_t * tiles, 8), rows_t * tiles)], local_sem.at[1]
     )
     own_b.start()
     own_t.start()
@@ -162,7 +173,7 @@
     own_t.wait()
 
     def relay(d):
-        for h in range(2):
+        for h in range(cuts):
             for from_left in (True, False):
                 if carried(d, h, from_left):
                     arrive(d, h, from_left)
@@ -191,10 +202,8 @@
     early = max(1, reach - 2)
     for d in range(1, early + 1):
         relay(d)
-        if d <= parts:
-            t_relay(d - 1)
-    for s in range(min(early, parts), parts):
-        t_relay(s)
+        for s in range(parts * (d - 1) // early, parts * d // early):
+            t_relay(s)
     for e in range(chips):
         for s in range(parts):
             landed(
@@ -205,9 +214,11 @@
     @pl.loop(0, width // 128)
     def _(i):
         rows = pl.ds(pl.multiple_of(i * 128, 128), 128)
-        high, low = split(t_all[rows, :])
-        t_high[rows, :] = high.astype(BF16)
-        t_low[rows, :] = low.astype(BF16)
+        for k in range(tiles):
+            part = t_all[pl.ds(i * (128 * tiles) + k, 128, stride=tiles), :]
+            high, low = split(part)
+            t_high[rows, k * lanes:(k + 1) * lanes] = high.astype(BF16)
+            t_low[rows, k * lanes:(k + 1) * lanes] = low.astype(BF16)
 
     @pl.loop(-(early - 1), early)
     def _(i):
@@ -235,7 +246,7 @@
             b_low[rows, :] = low.astype(BF16)
 
     def second_product(owner, s):
-        high, low = split(g_all[t_rows(owner, s), :])
+        high, low = split(g_all[g_rows(owner, s), :])
         both = jnp.concatenate([high, low], axis=0).astype(BF16)
         main = lax.dot_general(both, b_high[...], NT, preferred_element_type=F32)
         rest = lax.dot_general(high.astype(BF16), b_low[...], NT, preferred_element_type=F32)
@@ -270,13 +281,17 @@
 
     @pl.loop(0, parts)
     def _(s):
-        out[pl.ds(pl.multiple_of(s * piece, 8), piece), :] = chip_sum(0, s)
+        kept[s] = chip_sum(0, s)
 
     for s in range(parts):
-        rows = pl.ds(s * piece, piece)
+        total = kept[s]
         for e in range(1, chips):
             p_cross(e, s).wait_recv()
-            out[rows, :] += sum_in[e - 1, s]
+            total += sum_in[e - 1, s]
+        for k in range(tiles):
+            out[pl.ds(s * piece * tiles + k, piece, stride=tiles), :] = (
+                total[:, k * lanes:(k + 1) * lanes]
+            )
 
     for copy in started:
         copy.wait_send()
@@ -292,24 +307,27 @@
     count_fit, rows_b, _ = fitting.shape
     assert pair_dev == 1 and count_fit == 1
     chips = n_aux // 2
-    parts = 2 if rows_t % 16 == 0 else 1
+    parts = PARTS if rows_t % (8 * PARTS) == 0 else 1
     piece = rows_t // parts
-    cut = rows_b // 16 * 8
+    cuts = CUTS
     reach = n // 2
+    lanes = 128
+    tiles = width // lanes
     dma = pltpu.SemaphoreType.DMA
     whole_f32 = pltpu.VMEM((width, width), F32)
     whole_bf16 = pltpu.VMEM((width, width), BF16)
     blocks = lambda k: pltpu.VMEM((k, parts, piece, width), F32)
     result = pl.pallas_call(
-        functools.partial(kernel, n, chips, parts, cut),
-        out_shape=jax.ShapeDtypeStruct((rows_t, width), F32),
+        functools.partial(kernel, n, chips, parts, cuts),
+        out_shape=jax.ShapeDtypeStruct((rows_t * tiles, lanes), F32),
         in_specs=[pl.BlockSpec(memory_space=pl.ANY)] * 2,
         out_specs=pl.BlockSpec(memory_space=pltpu.VMEM),
         scratch_shapes=[
-            whole_f32, whole_f32, whole_bf16, whole_bf16, whole_bf16, whole_bf16, whole_f32,
+            pltpu.VMEM((width * tiles, lanes), F32), whole_f32, whole_bf16, whole_bf16, whole_bf16, whole_bf16, whole_f32,
             blocks(chips), blocks(chips), blocks(chips - 1), blocks(chips - 1),
+            pltpu.VMEM((parts, piece, width), F32),
             dma((2,)),
-            dma((reach, 2)), dma((reach, 2)), dma((reach, 2)), dma((reach, 2)),
+            dma((reach, cuts)), dma((reach, cuts)), dma((reach, cuts)), dma((reach, cuts)),
             dma((chips - 1, parts)), dma((chips - 1, parts)),
             dma((chips, parts)), dma((chips, parts)),
             dma((chips, parts)), dma((chips, parts)),
@@ -318,7 +336,7 @@
         compiler_params=pltpu.CompilerParams(
             collective_id=0, has_side_effects=True, vmem_limit_bytes=60 << 20
         ),
-    )(amplitudes.reshape(rows_t, width), fitting.reshape(rows_b, width))
+    )(amplitudes.reshape(rows_t * tiles, lanes), fitting.reshape(rows_b, width))
     return result.reshape(rows_t, pair_dev, width)
 
 

time: 66.8 us -> 63.6 us (0.952)
  local copies, waits for them, and re-layouts: 4.92 us -> 2.57 us
  Pallas kernels: 61.7 us -> 60.8 us
    reshape x1 -> x0, local copies, waits for them, and re-layouts: 2.85 us -> none  [per_device(): return result.reshape(rows_t, pair_dev, width)]
    pallas_call x1, Pallas kernels: 61.7 us -> 60.8 us  [per_device(): pl.pallas_call(functools.partial(kernel, n, chips, parts, cuts), out_shap...]
where the time goes in v2:
time: 63.6 us; the launch traced here: 63.4 us
  Pallas kernels  60.8 us (96%)
  local copies, waits for them, and re-layouts  2.57 us (4%)
    pallas_call x1, Pallas kernels, per_device(): pl.pallas_call(functools.partial(kernel, n, chips, parts, cuts), out_shap...  60.8 us
    unnamed x1, local copies, waits for them, and re-layouts  2.57 us

profile of v2, /device:TPU:0, one launch (start us, length us, event | category | flops | bytes accessed | tf_op | source)
XLA Modules:
  0.0 63.4 jit_solution(6411972952476004911)
XLA Ops:
  0.0 60.8 %shard_map.28 = f32[1568,128]{1,0:T(8,128)} custom-call(f32[1568,128]{1,0:T(8,128)} %bitcast.4, f32[112,896]{1,0:T(8,128)} %bitcast.5), custom_call_target="tpu_custom_call" | custom-call | tf_op jit(solution)/shard_map/pallas_call | solution.py:320
  60.8 2.6 %copy.5 = f32[224,1,896]{2,1,0:T(1,128)} copy(f32[224,1,896]{2,1,0:T(1,128)} %bitcast.3) | data formatting | bytes 1605632

commit v3 on v2

--- a/solution.py
+++ b/solution.py
@@ -36,10 +36,10 @@
 
 def kernel(
     n, chips, parts, cuts,
-    t_in, b_in, out,
+    t_in, b_in, kept, received,
     t_all, b_all, t_high, t_low, b_high, b_low, g_all,
-    mate_out, mate_in, sum_out, sum_in, kept,
-    local_sem, right_send, right_recv, left_send, left_recv,
+    mate_out, mate_in, sum_out, kept_v,
+    local_sem, keep_sem, right_send, right_recv, left_send, left_recv,
     tx_send, tx_recv, tm_send, tm_recv, pm_send, pm_recv, px_send, px_recv,
 ):
     rows_b, width = b_in.shape
@@ -261,10 +261,17 @@
 
     def p_cross(e, s):
         return pltpu.make_async_remote_copy(
-            src_ref=sum_out.at[e - 1, s], dst_ref=sum_in.at[e - 1, s],
+            src_ref=sum_out.at[e - 1, s], dst_ref=received.at[e - 1, s],
             send_sem=px_send.at[e - 1, s], recv_sem=px_recv.at[e - 1, s],
             device_id=(pair, chip_at(e) * 2 + core), device_id_type=MESH,
         )
+
+    def keep(s):
+        return pltpu.make_async_copy(kept_v.at[s], kept.at[s], keep_sem.at[s])
+
+    def spread(ref, value):
+        for k in range(tiles):
+            ref[pl.ds(k, piece, stride=tiles), :] = value[:, k * lanes:(k + 1) * lanes]
 
     def chip_sum(e, s):
         mate_out[e, s] = second_product(chip_at(e) * 2 + (1 - core), s)
@@ -276,22 +283,18 @@
     @pl.loop(0, (chips - 1) * parts)
     def _(i):
         e, s = i // parts + 1, i % parts
-        sum_out[e - 1, s] = chip_sum(e, s)
+        spread(sum_out.at[e - 1, s], chip_sum(e, s))
         p_cross(e, s).start()
 
     @pl.loop(0, parts)
     def _(s):
-        kept[s] = chip_sum(0, s)
+        spread(kept_v.at[s], chip_sum(0, s))
+        keep(s).start()
 
     for s in range(parts):
-        total = kept[s]
+        keep(s).wait()
         for e in range(1, chips):
             p_cross(e, s).wait_recv()
-            total += sum_in[e - 1, s]
-        for k in range(tiles):
-            out[pl.ds(s * piece * tiles + k, piece, stride=tiles), :] = (
-                total[:, k * lanes:(k + 1) * lanes]
-            )
 
     for copy in started:
         copy.wait_send()
@@ -316,17 +319,18 @@
     dma = pltpu.SemaphoreType.DMA
     whole_f32 = pltpu.VMEM((width, width), F32)
     whole_bf16 = pltpu.VMEM((width, width), BF16)
+    flat = (parts, piece * tiles, lanes)
     blocks = lambda k: pltpu.VMEM((k, parts, piece, width), F32)
-    result = pl.pallas_call(
+    kept, received = pl.pallas_call(
         functools.partial(kernel, n, chips, parts, cuts),
-        out_shape=jax.ShapeDtypeStruct((rows_t * tiles, lanes), F32),
+        out_shape=[jax.ShapeDtypeStruct(flat, F32), jax.ShapeDtypeStruct((chips - 1,) + flat, F32)],
         in_specs=[pl.BlockSpec(memory_space=pl.ANY)] * 2,
-        out_specs=pl.BlockSpec(memory_space=pltpu.VMEM),
+        out_specs=[pl.BlockSpec(memory_space=pl.ANY)] * 2,
         scratch_shapes=[
             pltpu.VMEM((width * tiles, lanes), F32), whole_f32, whole_bf16, whole_bf16, whole_bf16, whole_bf16, whole_f32,
-            blocks(chips), blocks(chips), blocks(chips - 1), blocks(chips - 1),
-            pltpu.VMEM((parts, piece, width), F32),
-            dma((2,)),
+            blocks(chips), blocks(chips),
+            pltpu.VMEM((chips - 1,) + flat, F32), pltpu.VMEM(flat, F32),
+            dma((2,)), dma((parts,)),
             dma((reach, cuts)), dma((reach, cuts)), dma((reach, cuts)), dma((reach, cuts)),
             dma((chips - 1, parts)), dma((chips - 1, parts)),
             dma((chips, parts)), dma((chips, parts)),
@@ -337,7 +341,9 @@
             collective_id=0, has_side_effects=True, vmem_limit_bytes=60 << 20
         ),
     )(amplitudes.reshape(rows_t * tiles, lanes), fitting.reshape(rows_b, width))
-    return result.reshape(rows_t, pair_dev, width)
+    for e in range(chips - 1):
+        kept = kept + received[e]
+    return kept.reshape(rows_t, pair_dev, width)
 
 
 def solution(mesh):

time: 63.6 us -> 62.5 us (0.983)
  local copies, waits for them, and re-layouts: 2.57 us -> 0 us
  other arithmetic: 0 us -> 2.35 us
  Pallas kernels: 60.8 us -> 60 us
    unnamed x1 -> x0, local copies, waits for them, and re-layouts: 2.57 us -> none
    add x0 -> x1, other arithmetic: none -> 2.35 us  [per_device(): kept = kept + received[e]]
    pallas_call x1, Pallas kernels: 60.8 us -> 60 us  [per_device(): pl.pallas_call(functools.partial(kernel, n, chips, parts, cuts), out_shap...]
where the time goes in v3:
time: 62.5 us; the launch traced here: 62.4 us
  Pallas kernels  60 us (96%)
  other arithmetic  2.35 us (4%)
    pallas_call x1, Pallas kernels, per_device(): pl.pallas_call(functools.partial(kernel, n, chips, parts, cuts), out_shap...  60 us
    add x1, other arithmetic, per_device(): kept = kept + received[e]  2.35 us

profile of v3, /device:TPU:0, one launch (start us, length us, event | category | flops | bytes accessed | tf_op | source)
XLA Modules:
  0.0 62.4 jit_solution(1552363179422869639)
XLA Ops:
  0.0 60.0 %shard_map.28 = (f32[4,392,128]{2,1,0:T(8,128)}, f32[1,4,392,128]{3,2,1,0:T(8,128)}) custom-call(f32[1568,128]{1,0:T(8,128)} %bitcast.5, f32[112,896]{1,0:T(8,128)} %bitcast.6), custom_call_target="tpu_custom_call" | custom-call | tf_op jit(solution)/shard_map/pallas_call | solution.py:324
  60.0 2.3 %bitcast_add_fusion = f32[4,392,128]{2,1,0:T(8,128)} fusion(f32[4,392,128]{2,1,0:T(8,128)} %get-tuple-element.7, f32[1,4,392,128]{3,2,1,0:T(8,128)} %get-tuple-element.8), kind=kLoop, calls=%fused_computation | loop fusion | flops 200704 | bytes 2408448 | tf_op jit(solution)/shard_map/add | solution.py:345

commit v4 on v3

--- a/solution.py
+++ b/solution.py
@@ -188,10 +188,10 @@
             )
             go(t_mate(e, s))
 
-    def first_product(block):
+    def first_product(block, late=False):
         rows = pl.ds(pl.multiple_of(block * rows_b, 8), rows_b)
         high, low = split(b_all[rows, :])
-        if rows_b % 16 == 0:
+        if rows_b % 16 == 0 and not late:
             b_high[pl.ds(pl.multiple_of(block * rows_b, 16), rows_b), :] = high.astype(BF16)
             b_low[pl.ds(pl.multiple_of(block * rows_b, 16), rows_b), :] = low.astype(BF16)
         both = jnp.concatenate([high, low], axis=0).astype(BF16)
@@ -235,7 +235,15 @@
     if reach > 1:
         both_sides(reach - 1)
     relay(reach)
-    first_product(at(reach))
+    far = at(reach)
+    half = parts // 2 if rows_t == 2 * rows_b and rows_b % 16 == 0 and chips == 2 else 0
+    if half:
+        rows = pl.ds(pl.multiple_of(far * rows_b, 16), rows_b)
+        high, low = split(b_all[pl.ds(pl.multiple_of(far * rows_b, 8), rows_b), :])
+        b_high[rows, :] = high.astype(BF16)
+        b_low[rows, :] = low.astype(BF16)
+    else:
+        first_product(far)
 
     if rows_b % 16:
         @pl.loop(0, width // 128)
@@ -280,11 +288,21 @@
         p_mate(e, s).wait_recv()
         return mine + mate_in[e, s]
 
-    @pl.loop(0, (chips - 1) * parts)
-    def _(i):
-        e, s = i // parts + 1, i % parts
+    def cross(i):
+        e, s = i // parts + 1, lax.rem(i + half * (1 - far % 2), parts)
         spread(sum_out.at[e - 1, s], chip_sum(e, s))
         p_cross(e, s).start()
+
+    if half:
+        @pl.loop(0, half)
+        def _(i):
+            cross(i)
+
+        first_product(far, late=True)
+
+    @pl.loop(half, (chips - 1) * parts)
+    def _(i):
+        cross(i)
 
     @pl.loop(0, parts)
     def _(s):

time: 62.5 us -> 61.7 us (0.987)
  Pallas kernels: 60 us -> 59.2 us
    pallas_call x1, Pallas kernels: 60 us -> 59.2 us  [per_device(): pl.pallas_call(functools.partial(kernel, n, chips, parts, cuts), out_shap...]
where the time goes in v4:
time: 61.7 us; the launch traced here: 61.6 us
  Pallas kernels  59.2 us (96%)
  other arithmetic  2.35 us (4%)
    pallas_call x1, Pallas kernels, per_device(): pl.pallas_call(functools.partial(kernel, n, chips, parts, cuts), out_shap...  59.2 us
    add x1, other arithmetic, per_device(): kept = kept + received[e]  2.35 us

profile of v4, /device:TPU:0, one launch (start us, length us, event | category | flops | bytes accessed | tf_op | source)
XLA Modules:
  0.0 61.6 jit_solution(15116386734801409096)
XLA Ops:
  0.0 59.2 %shard_map.28 = (f32[4,392,128]{2,1,0:T(8,128)}, f32[1,4,392,128]{3,2,1,0:T(8,128)}) custom-call(f32[1568,128]{1,0:T(8,128)} %bitcast.5, f32[112,896]{1,0:T(8,128)} %bitcast.6), custom_call_target="tpu_custom_call" | custom-call | tf_op jit(solution)/shard_map/pallas_call | solution.py:342
  59.2 2.3 %bitcast_add_fusion = f32[4,392,128]{2,1,0:T(8,128)} fusion(f32[4,392,128]{2,1,0:T(8,128)} %get-tuple-element.7, f32[1,4,392,128]{3,2,1,0:T(8,128)} %get-tuple-element.8), kind=kLoop, calls=%fused_computation | loop fusion | flops 200704 | bytes 2408448 | tf_op jit(solution)/shard_map/add | solution.py:363
